TPU v7x, 256 devices: a whole 4x4x8 slice. The times are simulated.
256 devices in a mesh: attn: 32 (over y, z), proj: 8 (over x, core).
Axes of the slice: x: 4, y: 4, z: 8, core: 2. Of those that a mesh axis runs over, the one named last changes fastest.
Arguments:
- tokens: bfloat16 [16384, 4096], P('attn', 'proj'), may hold values from -6 to 6
- norm_gain: float32 [4096], replicated, may hold values from 0.1 to 1.9
- w_query: bfloat16 [4096, 4096], P(None, 'proj')
- w_key: bfloat16 [4096, 1024], P(None, 'proj')
- value_matrix: bfloat16 [4096, 1024], P(None, 'proj'), may hold values from -0.09375 to 0.09375
- doc_lengths: int32 [128], replicated, may hold values from 1 to 512, 16384 in all
- block_server: int32 [128], P('attn'), may hold values from 0 to 31, as said below
Outputs:
- attn_out: bfloat16 [16384, 4096], P('attn', 'proj')
- served_lse: float32 [128, 32, 128], P('attn', 'proj')
Inputs may be any that keep to these rules, and one draw needn't show every extreme that they name: `doc_lengths`: the lengths sum to 16384. `block_server`: query block b belongs to the micro-batch b // 4; every index of attn serves exactly 4 blocks, and at most one block of any one micro-batch.
All inputs are finite; a program needn't handle non-finite values.
Results may differ from a plain program's by a relative error of at most 0.0074.
Values may be sent and summed in bfloat16 or wider, within the bound.
A program may use at most 128 MiB of HBM per device.

v0:
```python
import jax
import jax.numpy as jnp
from jax import lax
from jax.sharding import PartitionSpec as P

HEAD = 128
QB = 128
NEG = -1e30
norm_eps = 1e-05


def shards(tokens, norm_gain, w_query, w_key, value_matrix, doc_lengths, block_server):
    rows = tokens.shape[0]
    model_width = w_query.shape[0]
    heads = w_query.shape[1] // HEAD
    blocks = rows // QB
    servers = lax.axis_size("attn")
    me = lax.axis_index("attn")
    wide = lax.all_gather(tokens, "proj", axis=1, tiled=True).astype(jnp.float32)
    scaled = (wide * norm_gain[None, :]).astype(jnp.bfloat16)
    squares = jnp.sum(wide * wide, axis=1, keepdims=True)
    inverse = lax.rsqrt(squares / model_width + norm_eps)
    dot = lambda w: (jnp.dot(scaled, w, preferred_element_type=jnp.float32) * inverse).astype(
        jnp.bfloat16
    )
    k = dot(w_key)
    v = dot(value_matrix)
    kv = jnp.concatenate([k, v], axis=1)
    prior = lax.ppermute(kv, "attn", [(i, (i + 1) % servers) for i in range(servers)])
    q = dot(w_query)
    allkv = jnp.concatenate([prior, kv], axis=0)
    starts = jnp.cumsum(doc_lengths) - doc_lengths
    extent = rows + QB
    outs, lses = ([], [])
    for b in range(blocks):
        pos = me * rows + b * QB + jnp.arange(QB, dtype=jnp.int32)
        first = jnp.max(jnp.where(starts[None, :] <= pos[:, None], starts[None, :], 0), axis=1)
        kpos = (me - 1) * rows + b * QB + jnp.arange(extent, dtype=jnp.int32)
        allowed = (kpos[None, :] >= first[:, None]) & (kpos[None, :] <= pos[:, None])
        win = allkv[b * QB : b * QB + extent]
        qb = q[b * QB : (b + 1) * QB].reshape(QB, heads, HEAD)
        s = jnp.einsum("qhd,kd->hqk", qb, win[:, :HEAD], preferred_element_type=jnp.float32)
        s = jnp.where(allowed, s * (1.0 / HEAD**0.5), NEG)
        m = jnp.max(s, axis=-1)
        w = jnp.where(allowed, jnp.exp(s - m[..., None]), 0.0)
        total = jnp.sum(w, axis=-1)
        o = jnp.einsum(
            "hqk,kd->hqd", w.astype(jnp.bfloat16), win[:, HEAD:], preferred_element_type=jnp.float32
        )
        o = (o / total[..., None]).transpose(1, 0, 2).reshape(QB, heads * HEAD).astype(jnp.bfloat16)
        outs.append(o)
        lses.append(m + jnp.log(total))
    attn_out = jnp.concatenate(outs, axis=0)
    lse = jnp.stack(lses)
    slot = jnp.arange(servers, dtype=jnp.int32)
    sending = block_server[None, :] == slot[:, None]
    send = jnp.sum(jnp.where(sending[:, :, None, None], lse[None], 0.0), axis=1)
    flag = jnp.any(sending, axis=1).astype(jnp.float32)
    send = jnp.concatenate([send, jnp.broadcast_to(flag[:, None, None], (servers, 1, QB))], axis=1)
    recv = lax.all_to_all(send, "attn", split_axis=0, concat_axis=0, tiled=True)
    valid = recv[:, heads, 0] > 0
    rank = jnp.cumsum(valid.astype(jnp.int32)) - 1
    pick = (rank[None, :] == jnp.arange(blocks, dtype=jnp.int32)[:, None]) & valid[None, :]
    served = jnp.sum(jnp.where(pick[:, :, None, None], recv[None, :, :heads], 0.0), axis=1)
    return (attn_out, served)


def solution(mesh):
    return jax.shard_map(
        shards,
        mesh=mesh,
        in_specs=(
            P("attn", "proj"),
            P(),
            P(None, "proj"),
            P(None, "proj"),
            P(None, "proj"),
            P(),
            P("attn"),
        ),
        out_specs=(P("attn", "proj"), P("attn", "proj", None)),
        check_vma=False,
    )
```

profile of v0, /device:TPU:32, one launch (start us, length us, event | category | flops | bytes accessed | tf_op | source)
XLA Modules:
  0.0 96.2 jit_solution(9389079406854169225)
XLA Ops:
  7.2 0.0 copy-start
  7.2 0.0 all-gather.2.cloned.1.call-start
  7.2 0.7 all-gather.2.cloned.1.call-update
  7.9 0.7 iota_compare_fusion.1
  8.7 0.8 copy.85
  9.4 0.2 reduce-window.17
  9.6 0.1 reduce
  9.7 0.7 sub.48
  10.5 0.2 select_reduce_fusion.5
  10.7 0.2 compare_and_fusion.2
  11.0 0.2 compare_and_fusion
  11.2 35.8 %all-gather.2.cloned.1.call-done = bf16[512,4096]{1,0:T(8,128)(2,1)} async-done(((bf16[512,512]{1,0:T(8,128)(2,1)}), bf16[512,4096]{1,0:T(8,128)(2,1)}) %all-gather.2.cloned.1.call-update) | async-done | bytes 4194320 | tf_op jit(solution)/shard_map/all_gather | solution.py:19
  47.0 3.2 %fusion.1 = f32[512]{0:T(512)S(1)} fusion(bf16[512,4096]{1,0:T(8,128)(2,1)} %all-gather.2.cloned.1.call-done), kind=kLoop, calls=%fused_computation.3 | loop fusion | flops 6290944 | bytes 4196352 | tf_op jit(solution)/shard_map/reduce_sum | solution.py:21
  50.3 0.2 copy-done.1
  50.5 1.5 %fusion.36 = bf16[512,128]{0,1:T(8,128)(2,1)S(1)} fusion(bf16[4096,128]{1,0:T(8,128)(2,1)S(1)} %copy-done, bf16[512,4096]{1,0:T(8,128)(2,1)S(1)} %copy-done.1, f32[4096]{0:T(1024)S(1)} %copy-done.4, f32[512]{0:T(512)S(1)} %add_rsqrt_fusion), kind=kOutput, calls=%fused_computation.39 | convolution fusion | flops 543293440 | bytes 5392384 | tf_op jit(solution)/shard_map/dot_general | solution.py:23
  52.0 0.0 copy-start.2
  52.0 1.5 %fusion.39 = bf16[512,128]{0,1:T(8,128)(2,1)S(1)} fusion(bf16[4096,128]{1,0:T(8,128)(2,1)S(1)} %copy-done.3, bf16[512,4096]{1,0:T(8,128)(2,1)S(1)} %copy-done.1, f32[4096]{0:T(1024)S(1)} %copy-done.4, f32[512]{0:T(512)S(1)} %add_rsqrt_fusion), kind=kOutput, calls=%fused_computation.40 | convolution fusion | flops 543293440 | bytes 5392384 | tf_op jit(solution)/shard_map/dot_general | solution.py:23
  53.6 1.6 %collective-permute-start = (bf16[512,256]{0,1:T(8,128)(2,1)S(1)}, bf16[512,256]{0,1:T(8,128)(2,1)S(1)}, u32[]{:S(2)}, u32[]{:S(2)}) collective-permute-start(bf16[512,256]{0,1:T(8,128)(2,1)S(1)} %pad_maximum_fusion.1), channel_id=1, source_target_pairs={{0,8},{8,16},{16,24},{24,32},{32,40},{40,48},{48,56},{56,64},{64,7... | collective-permute-start | bytes 786440 | tf_op jit(solution)/shard_map/ppermute | solution.py:29
  55.2 2.4 %fusion.19 = bf16[512,512]{0,1:T(8,128)(2,1)S(1)} fusion(bf16[4096,512]{1,0:T(8,128)(2,1)S(1)} %copy-done.2, bf16[512,4096]{1,0:T(8,128)(2,1)S(1)} %copy-done.1, f32[4096]{0:T(1024)S(1)} %copy-done.4, f32[512]{0:T(512)S(1)} %add_rsqrt_fusion), kind=kOutput, calls=%fused_computation.24 | convolution fusion | flops 2154299392 | bytes 8931328 | tf_op jit(solution)/shard_map/dot_general | solution.py:23
  57.7 0.1 fusion.72
  57.8 4.4 %collective-permute-done = bf16[512,256]{0,1:T(8,128)(2,1)S(1)} collective-permute-done((bf16[512,256]{0,1:T(8,128)(2,1)S(1)}, bf16[512,256]{0,1:T(8,128)(2,1)S(1)}, u32[]{:S(2)}, u32[]{:S(2)}) %collective-permute-start) | collective-permute-done | bytes 262176 | tf_op jit(solution)/shard_map/ppermute | solution.py:29
  62.1 0.1 maximum_maximum_fusion
  62.2 0.4 fusion.73
  62.6 0.3 fusion.48
  62.8 0.4 fusion.35
  63.2 0.4 fusion.74
  63.6 0.3 fusion.46
  63.9 0.4 fusion.34
  64.2 0.4 fusion.75
  64.6 0.3 fusion.44
  64.9 0.4 fusion.33
  65.2 0.4 fusion.76
  65.6 0.3 fusion.42
  65.9 0.1 select_reduce_fusion.1
  66.0 0.1 broadcast_in_dim.155
  66.1 0.7 copy.102
  66.8 11.3 %all-to-all-start = ((f32[32,5,128]{2,1,0:T(8,128)}), f32[32,5,128]{2,1,0:T(8,128)S(1)}, u32[]{:S(2)}, u32[]{:S(2)}) async-start(f32[32,5,128]{2,1,0:T(8,128)} %copy.102), calls=%async_computation | async-start | bytes 262144 | tf_op jit(solution)/shard_map/all_to_all | solution.py:60
  78.1 1.0 %fusion.32 = bf16[128,4,128]{0,2,1:T(8,128)(2,1)} fusion(f32[4,128,640]{1,2,0:T(8,128)S(1)} %get-tuple-element.21, f32[4,128]{1,0:T(4,128)S(1)} %get-tuple-element.20, pred[128,640]{0,1:T(8,128)(4,1)S(1)} %get-tuple-element.25, bf16[1024,256]{0,1:T(8,128)(2,1)S(1)} %maximum_maximum_fusion, f32[128,4]{0,1:T(4,128)S(1)} %bitcast.110), kind=kOutput, calls=%fused_computation.35 | convolution fusion | flops 85000192 | bytes 1691648 | tf_op jit(solution)/shard_map/hqk,kd->hqd/dot_general | solution.py:47
  79.1 0.1 copy.101
  79.2 0.1 copy.100
  79.3 0.1 copy.99
  79.4 1.0 %copy.98 = bf16[128,512]{1,0:T(8,128)(2,1)S(1)} copy(bf16[128,512]{0,1:T(8,128)(2,1)} %bitcast.104) | data formatting | bytes 262144 | tf_op jit(solution)/shard_map/convert_element_type | solution.py:50
  80.4 0.8 pad_maximum_fusion
  81.3 6.4 %all-to-all-done = f32[32,5,128]{2,1,0:T(8,128)S(1)} async-done(((f32[32,5,128]{2,1,0:T(8,128)}), f32[32,5,128]{2,1,0:T(8,128)S(1)}, u32[]{:S(2)}, u32[]{:S(2)}) %all-to-all-start) | async-done | bytes 81952 | tf_op jit(solution)/shard_map/all_to_all | solution.py:60
  87.8 0.7 compare_reduce_fusion
  88.4 0.1 reduce-window.18
  88.5 0.1 add_reduce_fusion
  88.6 0.7 select_reduce_fusion
  (27 shorter events, 0.2 us)
Async XLA Ops:
  7.2 43.1 %copy-start = (bf16[4096,128]{1,0:T(8,128)(2,1)S(1)}, bf16[4096,128]{1,0:T(8,128)(2,1)}, u32[]{:S(2)}) copy-start(bf16[4096,128]{1,0:T(8,128)(2,1)} %param.11) | copy-start | bytes 3145732
  7.2 39.9 %all-gather.2.cloned.1.call-start = ((), (), s32[]{:S(2)}) async-start(), calls=%async_computation.1 | async-start | bytes 4718592 | tf_op jit(solution)/shard_map/all_gather | solution.py:19
  11.0 39.3 %copy-start.4 = (f32[4096]{0:T(1024)S(1)}, f32[4096]{0:T(1024)}, u32[]{:S(2)}) copy-start(f32[4096]{0:T(1024)} %param.8) | copy-start | bytes 49156
  47.0 3.4 %copy-start.1 = (bf16[512,4096]{1,0:T(8,128)(2,1)S(1)}, bf16[512,4096]{1,0:T(8,128)(2,1)}, u32[]{:S(2)}) copy-start(bf16[512,4096]{1,0:T(8,128)(2,1)} %all-gather.2.cloned.1.call-done) | copy-start | bytes 12582916
  50.5 1.5 %copy-start.3 = (bf16[4096,128]{1,0:T(8,128)(2,1)S(1)}, bf16[4096,128]{1,0:T(8,128)(2,1)}, u32[]{:S(2)}) copy-start(bf16[4096,128]{1,0:T(8,128)(2,1)} %param.10) | copy-start | bytes 3145732
  52.0 3.2 %copy-start.2 = (bf16[4096,512]{1,0:T(8,128)(2,1)S(1)}, bf16[4096,512]{1,0:T(8,128)(2,1)}, u32[]{:S(2)}) copy-start(bf16[4096,512]{1,0:T(8,128)(2,1)} %param.9) | copy-start | bytes 12582916
  53.6 8.5 %collective-permute-start = (bf16[512,256]{0,1:T(8,128)(2,1)S(1)}, bf16[512,256]{0,1:T(8,128)(2,1)S(1)}, u32[]{:S(2)}, u32[]{:S(2)}) collective-permute-start(bf16[512,256]{0,1:T(8,128)(2,1)S(1)} %pad_maximum_fusion.1), channel_id=1, source_target_pairs={{0,8},{8,16},{16,24},{24,32},{32,40},{40,48},{48,56},{56,64},{64,7... | collective-permute-start | bytes 786440 | tf_op jit(solution)/shard_map/ppermute | solution.py:29
  66.8 21.0 %all-to-all-start = ((f32[32,5,128]{2,1,0:T(8,128)}), f32[32,5,128]{2,1,0:T(8,128)S(1)}, u32[]{:S(2)}, u32[]{:S(2)}) async-start(f32[32,5,128]{2,1,0:T(8,128)} %copy.102), calls=%async_computation | async-start | bytes 262144 | tf_op jit(solution)/shard_map/all_to_all | solution.py:60
Sparse Core Ops, SparseCore 0:
  9.8 37.1 all-gather.1
where the time goes:
time: 96.4 us; the launch traced here: 96.2 us
  waiting for transfers between devices  47.3 us (49%)
  between operations  14.4 us (15%)
  starting transfers between devices  13 us (13%)
  other arithmetic  9.3 us (10%)
  matrix products  9.06 us (9%)
  local copies, waits for them, and re-layouts  3.2 us (3%)
    all_gather x1, waiting for transfers between devices, shards(): lax.all_gather(tokens, 'proj', axis=1, tiled=True).astype(jnp.float32)  35.8 us
    all_to_all x1, starting transfers between devices, shards(): recv = lax.all_to_all(send, 'attn', split_axis=0, concat_axis=0, tiled=True)  11.3 us
    all_to_all x1, waiting for transfers between devices, shards(): recv = lax.all_to_all(send, 'attn', split_axis=0, concat_axis=0, tiled=True)  6.45 us
    dot_general x3, matrix products, shards(): jnp.dot(scaled, w, preferred_element_type=jnp.float32) * inverse  5.48 us
    ppermute x1, waiting for transfers between devices, shards(): lax.ppermute(kv, 'attn', [(i, (i + 1) % servers) for i in range(servers)])  4.36 us
    reduce_sum x1, other arithmetic, shards(): squares = jnp.sum(wide * wide, axis=1, keepdims=True)  3.23 us
    dot_general x4, matrix products, shards(): jnp.einsum('hqk,kd->hqd', w.astype(jnp.bfloat16), win[:, HEAD:], preferre...  2.09 us
  transfers between devices with their start and end apart: 3, of which 3 were waited for; matrix products, arithmetic and copies ran while one was open for 9% of the time, Pallas kernels for 0%

commit v1 on v0

--- a/solution.py
+++ b/solution.py
@@ -16,7 +16,9 @@
     blocks = rows // QB
     servers = lax.axis_size("attn")
     me = lax.axis_index("attn")
-    wide = lax.all_gather(tokens, "proj", axis=1, tiled=True).astype(jnp.float32)
+    wide = jnp.concatenate(
+        lax.all_to_all(jnp.stack([tokens] * lax.axis_size("proj")), "proj", 0, 0), axis=1
+    ).astype(jnp.float32)
     scaled = (wide * norm_gain[None, :]).astype(jnp.bfloat16)
     squares = jnp.sum(wide * wide, axis=1, keepdims=True)
     inverse = lax.rsqrt(squares / model_width + norm_eps)

time: 96.4 us -> 103 us (1.068)
  between operations: 14.4 us -> 0.99 us
  waiting for transfers between devices: 47.3 us -> 58.1 us
  starting transfers between devices: 13 us -> 19.2 us
  local copies, waits for them, and re-layouts: 3.2 us -> 6.42 us
  matrix products: 9.06 us -> 7.6 us
  other arithmetic: 9.3 us -> 10.6 us
    all_to_all x0 -> x1, waiting for transfers between devices: none -> 48.3 us  [shards(): lax.all_to_all(jnp.stack([tokens] * lax.axis_size('proj')), 'proj', 0, 0)]
    all_gather x1 -> x0, waiting for transfers between devices: 35.8 us -> none  [shards(): lax.all_gather(tokens, 'proj', axis=1, tiled=True).astype(jnp.float32)]
    all_to_all x0 -> x1, starting transfers between devices: none -> 4.68 us  [shards(): lax.all_to_all(jnp.stack([tokens] * lax.axis_size('proj')), 'proj', 0, 0)]
    convert_element_type x0 -> x1, other arithmetic: none -> 2.71 us  [shards(): scaled = (wide * norm_gain[None, :]).astype(jnp.bfloat16)]
    another operation x1 -> x2, local copies, waits for them, and re-layouts: 0.76 us -> 2.44 us  [the longest x1 2.33 us: shards(): jnp.stack([tokens] * lax.axis_size('proj'))]
    unnamed x10 -> x13, local copies, waits for them, and re-layouts: 0.22 us -> 1.75 us
    dot_general x3, matrix products: 5.48 us -> 4.03 us  [shards(): jnp.dot(scaled, w, preferred_element_type=jnp.float32) * inverse]
    all_to_all x1, starting transfers between devices: 11.3 us -> 12.5 us  [shards(): recv = lax.all_to_all(send, 'attn', split_axis=0, concat_axis=0, tiled=True)]
  transfers between devices with their start and end apart: 3 -> 3, of which waited for: 3 -> 3; matrix products, arithmetic and copies ran while one was open for 9% -> 7% of each run, Pallas kernels for 0% -> 0%
where the time goes in v1:
time: 103 us
  waiting for transfers between devices  58.1 us (56%)
  starting transfers between devices  19.2 us (19%)
  other arithmetic  10.6 us (10%)
  matrix products  7.6 us (7%)
  local copies, waits for them, and re-layouts  6.42 us (6%)
    all_to_all x1, waiting for transfers between devices, shards(): lax.all_to_all(jnp.stack([tokens] * lax.axis_size('proj')), 'proj', 0, 0)  48.3 us
    all_to_all x1, starting transfers between devices, shards(): recv = lax.all_to_all(send, 'attn', split_axis=0, concat_axis=0, tiled=True)  12.5 us
    all_to_all x1, waiting for transfers between devices, shards(): recv = lax.all_to_all(send, 'attn', split_axis=0, concat_axis=0, tiled=True)  6.45 us
    all_to_all x1, starting transfers between devices, shards(): lax.all_to_all(jnp.stack([tokens] * lax.axis_size('proj')), 'proj', 0, 0)  4.68 us
    dot_general x3, matrix products, shards(): jnp.dot(scaled, w, preferred_element_type=jnp.float32) * inverse  4.03 us
    ppermute x1, waiting for transfers between devices, shards(): lax.ppermute(kv, 'attn', [(i, (i + 1) % servers) for i in range(servers)])  3.43 us
    reduce_sum x1, other arithmetic, shards(): squares = jnp.sum(wide * wide, axis=1, keepdims=True)  3.14 us
    convert_element_type x1, other arithmetic, shards(): scaled = (wide * norm_gain[None, :]).astype(jnp.bfloat16)  2.71 us
  transfers between devices with their start and end apart: 3, of which 3 were waited for; matrix products, arithmetic and copies ran while one was open for 7% of the time, Pallas kernels for 0%

profile of v1, /device:TPU:32, one launch (start us, length us, event | category | flops | bytes accessed | tf_op | source)
XLA Modules:
  0.0 102.9 jit_solution(13829106182458820553)
XLA Ops:
  0.6 0.0 copy-start
  0.6 1.3 %copy.89 = bf16[512,512]{0,1:T(8,128)(2,1)S(1)} copy(bf16[512,512]{1,0:T(8,128)(2,1)} %param.7) | data formatting | bytes 1048576 | tf_op args[0]
  2.0 2.3 %stack.4 = bf16[8,512,512]{1,2,0:T(8,128)(2,1)} broadcast(bf16[512,512]{0,1:T(8,128)(2,1)S(1)} %copy.89), dimensions={1,2} | broadcast | bytes 4718592 | tf_op jit(solution)/shard_map/stack | solution.py:20
  4.3 4.7 %all-to-all-start = ((bf16[8,512,512]{1,2,0:T(8,128)(2,1)}), bf16[8,512,512]{1,2,0:T(8,128)(2,1)}, u32[]{:S(2)}, u32[]{:S(2)}) async-start(bf16[8,512,512]{1,2,0:T(8,128)(2,1)} %stack.4), calls=%async_computation | async-start | bytes 8388608 | tf_op jit(solution)/shard_map/all_to_all | solution.py:20
  9.0 0.1 copy.88
  9.1 0.2 reduce-window.17
  9.3 0.1 reduce.2
  9.4 0.1 iota_compare_fusion.1
  9.6 0.2 select_reduce_fusion.5
  9.9 0.2 compare_and_fusion
  10.1 0.2 compare_and_fusion.2
  10.4 48.3 %all-to-all-done = bf16[8,512,512]{1,2,0:T(8,128)(2,1)} async-done(((bf16[8,512,512]{1,2,0:T(8,128)(2,1)}), bf16[8,512,512]{1,2,0:T(8,128)(2,1)}, u32[]{:S(2)}, u32[]{:S(2)}) %all-to-all-start) | async-done | bytes 4194336 | tf_op jit(solution)/shard_map/all_to_all | solution.py:20
  58.6 3.1 %multiply_reduce_fusion = f32[512]{0:T(512)S(1)} fusion(bf16[8,512,512]{1,2,0:T(8,128)(2,1)} %all-to-all-done), kind=kLoop, calls=%fused_computation.2 | loop fusion | flops 6290944 | bytes 4196352 | tf_op jit(solution)/shard_map/reduce_sum | solution.py:23
  61.8 2.7 %fusion = bf16[512,4096]{0,1:T(8,128)(2,1)S(1)} fusion(f32[4096]{0:T(1024)S(1)} %copy-done.1, bf16[8,512,512]{1,2,0:T(8,128)(2,1)} %all-to-all-done), kind=kLoop, calls=%fused_computation.1 | loop fusion | flops 6291456 | bytes 8404992 | tf_op jit(solution)/shard_map/convert_element_type | solution.py:22
  64.5 0.8 fusion.19
  65.4 0.4 copy-done.4
  65.8 0.8 fusion.18
  66.6 2.0 %collective-permute-start = (bf16[512,256]{0,1:T(8,128)(2,1)S(1)}, bf16[512,256]{0,1:T(8,128)(2,1)S(1)}, u32[]{:S(2)}, u32[]{:S(2)}) collective-permute-start(bf16[512,256]{0,1:T(8,128)(2,1)S(1)} %pad_maximum_fusion.1), channel_id=1, source_target_pairs={{0,8},{8,16},{16,24},{24,32},{32,40},{40,48},{48,56},{56,64},{64,7... | collective-permute-start | bytes 786440 | tf_op jit(solution)/shard_map/ppermute | solution.py:31
  68.6 2.4 %fusion.9 = bf16[512,512]{0,1:T(8,128)(2,1)S(1)} fusion(bf16[512,4096]{0,1:T(8,128)(2,1)S(1)} %fusion, bf16[4096,512]{1,0:T(8,128)(2,1)S(1)} %copy-done.3, f32[512]{0:T(512)S(1)} %add_rsqrt_fusion), kind=kOutput, calls=%fused_computation.20 | convolution fusion | flops 2148007936 | bytes 8914944 | tf_op jit(solution)/shard_map/dot_general | solution.py:25
  71.0 0.1 fusion.50
  71.1 3.4 %collective-permute-done = bf16[512,256]{0,1:T(8,128)(2,1)S(1)} collective-permute-done((bf16[512,256]{0,1:T(8,128)(2,1)S(1)}, bf16[512,256]{0,1:T(8,128)(2,1)S(1)}, u32[]{:S(2)}, u32[]{:S(2)}) %collective-permute-start) | collective-permute-done | bytes 262176 | tf_op jit(solution)/shard_map/ppermute | solution.py:31
  74.5 0.1 maximum_maximum_fusion
  74.6 0.4 fusion.51
  75.0 0.3 fusion.26
  75.2 0.4 fusion.17
  75.6 0.4 fusion.52
  76.0 0.3 fusion.24
  76.2 0.4 fusion.16
  76.6 0.4 fusion.53
  77.0 0.3 fusion.22
  77.2 0.4 fusion.15
  77.6 0.4 fusion.54
  78.0 0.3 fusion.20
  78.3 0.1 select_reduce_fusion.1
  78.4 0.1 broadcast_in_dim.155
  78.5 0.7 copy.106
  79.1 12.5 %all-to-all-start.1 = ((f32[32,5,128]{2,1,0:T(8,128)}), f32[32,5,128]{2,1,0:T(8,128)S(1)}, u32[]{:S(2)}, u32[]{:S(2)}) async-start(f32[32,5,128]{2,1,0:T(8,128)} %copy.106), calls=%async_computation.1 | async-start | bytes 262144 | tf_op jit(solution)/shard_map/all_to_all | solution.py:62
  91.6 1.0 fusion.14
  92.7 0.1 copy.105
  92.8 0.1 copy.104
  92.9 0.1 copy.103
  93.0 1.0 copy.102
  94.0 0.8 pad_maximum_fusion
  94.9 6.4 %all-to-all-done.1 = f32[32,5,128]{2,1,0:T(8,128)S(1)} async-done(((f32[32,5,128]{2,1,0:T(8,128)}), f32[32,5,128]{2,1,0:T(8,128)S(1)}, u32[]{:S(2)}, u32[]{:S(2)}) %all-to-all-start.1) | async-done | bytes 81952 | tf_op jit(solution)/shard_map/all_to_all | solution.py:62
  101.3 0.7 compare_reduce_fusion
  102.0 0.1 reduce-window.18
  102.1 0.1 add_reduce_fusion
  102.2 0.7 select_reduce_fusion
  (31 shorter events, 0.2 us)
Async XLA Ops:
  0.6 63.9 %copy-start = (bf16[4096,128]{1,0:T(8,128)(2,1)S(1)}, bf16[4096,128]{1,0:T(8,128)(2,1)}, u32[]{:S(2)}) copy-start(bf16[4096,128]{1,0:T(8,128)(2,1)} %param.11) | copy-start | bytes 3145732
  4.3 4.7 %copy-start.2 = (s32[128]{0:T(128)S(1)}, s32[128]{0:T(128)}, u32[]{:S(2)}) copy-start(s32[128]{0:T(128)} %param.12) | copy-start | bytes 1540
  4.3 5.1 %copy-start.5 = (s32[4]{0:T(128)S(1)}, s32[4]{0:T(128)}, u32[]{:S(2)}) copy-start(s32[4]{0:T(128)} %param.13) | copy-start | bytes 52
  4.3 54.3 %all-to-all-start = ((bf16[8,512,512]{1,2,0:T(8,128)(2,1)}), bf16[8,512,512]{1,2,0:T(8,128)(2,1)}, u32[]{:S(2)}, u32[]{:S(2)}) async-start(bf16[8,512,512]{1,2,0:T(8,128)(2,1)} %stack.4), calls=%async_computation | async-start | bytes 8388608 | tf_op jit(solution)/shard_map/all_to_all | solution.py:20
  10.4 51.4 %copy-start.1 = (f32[4096]{0:T(1024)S(1)}, f32[4096]{0:T(1024)}, u32[]{:S(2)}) copy-start(f32[4096]{0:T(1024)} %param.8) | copy-start | bytes 49156
  64.5 1.2 %copy-start.4 = (bf16[4096,128]{1,0:T(8,128)(2,1)S(1)}, bf16[4096,128]{1,0:T(8,128)(2,1)}, u32[]{:S(2)}) copy-start(bf16[4096,128]{1,0:T(8,128)(2,1)} %param.10) | copy-start | bytes 3145732
  65.8 2.9 %copy-start.3 = (bf16[4096,512]{1,0:T(8,128)(2,1)S(1)}, bf16[4096,512]{1,0:T(8,128)(2,1)}, u32[]{:S(2)}) copy-start(bf16[4096,512]{1,0:T(8,128)(2,1)} %param.9) | copy-start | bytes 12582916
  66.6 7.9 %collective-permute-start = (bf16[512,256]{0,1:T(8,128)(2,1)S(1)}, bf16[512,256]{0,1:T(8,128)(2,1)S(1)}, u32[]{:S(2)}, u32[]{:S(2)}) collective-permute-start(bf16[512,256]{0,1:T(8,128)(2,1)S(1)} %pad_maximum_fusion.1), channel_id=1, source_target_pairs={{0,8},{8,16},{16,24},{24,32},{32,40},{40,48},{48,56},{56,64},{64,7... | collective-permute-start | bytes 786440 | tf_op jit(solution)/shard_map/ppermute | solution.py:31
  79.1 22.2 %all-to-all-start.1 = ((f32[32,5,128]{2,1,0:T(8,128)}), f32[32,5,128]{2,1,0:T(8,128)S(1)}, u32[]{:S(2)}, u32[]{:S(2)}) async-start(f32[32,5,128]{2,1,0:T(8,128)} %copy.106), calls=%async_computation.1 | async-start | bytes 262144 | tf_op jit(solution)/shard_map/all_to_all | solution.py:62
